TPU v7x, 32 devices: a whole 2x2x4 slice. The times are simulated.
32 devices in a mesh: gy: 4 (over y, x), gz: 8 (over z, core).
Axes of the slice: x: 2, y: 2, z: 4, core: 2. Of those that a mesh axis runs over, the one named last changes fastest.
Arguments:
- conduct: float32 [64, 256, 128], P('gy', 'gz'), may hold values from 0.3 to 3
- seeds: int32 [64, 256, 128], P('gy', 'gz'), may hold values 0 or 1
- labels: int32 [64, 256, 128], P('gy', 'gz'), may hold values 0 or 1
- start: float32 [64, 256, 128], P('gy', 'gz'), may hold values from 0 to 1
- cotangent: float32 [64, 256, 128], P('gy', 'gz'), may hold values from -12 to 12
Outputs:
- probability: float32 [64, 256, 128], P('gy', 'gz')
- adjoint: float32 [64, 256, 128], P('gy', 'gz')
- grad_conduct: float32 [64, 256, 128], P('gy', 'gz')
All inputs are finite; a program needn't handle non-finite values. No bound on the sum of `seeds` or of `labels` on one device may be relied on, other than what follows from the above.
Results may differ from a plain program's by a relative error of at most 0.0001.
Values sent between devices are 32-bit elements; how exact they have to be, the bound alone decides.
A program may use at most 64 MiB of HBM per device.

v0:
```python
import jax
import jax.numpy as jnp
from jax import lax
from jax.sharding import PartitionSpec as P

ITERS = 2
seed_pull = 4.0
screening = 0.05


def with_halo(block, sides, width):
    for axis, dim in sides:
        count = lax.axis_size(axis)
        forward = [(i, i + 1) for i in range(count - 1)]
        backward = [(target, source) for source, target in forward]
        low = lax.ppermute(
            lax.slice_in_dim(block, block.shape[dim] - width, None, axis=dim), axis, forward
        )
        high = lax.ppermute(lax.slice_in_dim(block, 0, width, axis=dim), axis, backward)
        block = jnp.concatenate([low, block, high], axis=dim)
    return block


def harmonic(first, second):
    return 2.0 * first * second / (first + second)


def faces(field):
    return with_halo(field, (("gy", 0), ("gz", 1)), 1)


def coefficients(padded_cond, seeds):
    core = padded_cond[1:-1, 1:-1]
    along = jnp.pad(core, ((0, 0), (0, 0), (1, 1)))
    weights = (
        harmonic(core, padded_cond[2:, 1:-1]),
        harmonic(core, padded_cond[:-2, 1:-1]),
        harmonic(core, padded_cond[1:-1, 2:]),
        harmonic(core, padded_cond[1:-1, :-2]),
        harmonic(core, along[..., 2:]),
        harmonic(core, along[..., :-2]),
    )
    diagonal = weights[0] + weights[1] + weights[2] + weights[3] + weights[4] + weights[5]
    diagonal = diagonal + seed_pull * seeds.astype(jnp.float32) + screening
    return (diagonal,) + weights


def operate(padded, coeffs):
    field = padded[1:-1, 1:-1]
    along = jnp.pad(field, ((0, 0), (0, 0), (1, 1)))
    out = coeffs[0] * field - coeffs[1] * padded[2:, 1:-1] - coeffs[2] * padded[:-2, 1:-1]
    out = out - coeffs[3] * padded[1:-1, 2:] - coeffs[4] * padded[1:-1, :-2]
    return out - coeffs[5] * along[..., 2:] - coeffs[6] * along[..., :-2]


def edge_term(ci, cj, ui, uj, vi, vj):
    total = ci + cj
    return -2.0 * cj * cj / (total * total) * (ui - uj) * (vi - vj)


def gradient(cond_pad, prob_pad, adj_pad):
    ci = cond_pad[1:-1, 1:-1]
    ui = prob_pad[1:-1, 1:-1]
    vi = adj_pad[1:-1, 1:-1]
    out = edge_term(ci, cond_pad[2:, 1:-1], ui, prob_pad[2:, 1:-1], vi, adj_pad[2:, 1:-1])
    out = out + edge_term(ci, cond_pad[:-2, 1:-1], ui, prob_pad[:-2, 1:-1], vi, adj_pad[:-2, 1:-1])
    out = out + edge_term(ci, cond_pad[1:-1, 2:], ui, prob_pad[1:-1, 2:], vi, adj_pad[1:-1, 2:])
    out = out + edge_term(ci, cond_pad[1:-1, :-2], ui, prob_pad[1:-1, :-2], vi, adj_pad[1:-1, :-2])
    cx = jnp.pad(ci, ((0, 0), (0, 0), (1, 1)))
    ux = jnp.pad(ui, ((0, 0), (0, 0), (1, 1)))
    vx = jnp.pad(vi, ((0, 0), (0, 0), (1, 1)))
    out = out + edge_term(ci, cx[..., 2:], ui, ux[..., 2:], vi, vx[..., 2:])
    return out + edge_term(ci, cx[..., :-2], ui, ux[..., :-2], vi, vx[..., :-2])


def paired_sums(resid, image):
    return lax.psum((jnp.sum(resid * resid), jnp.sum(resid * image)), ("gy", "gz"))


def conjugate(iterate, iterate_pad, resid, coeffs):
    resid_pad = faces(resid)
    image = operate(resid_pad, coeffs)
    norm_now, product = paired_sums(resid, image)
    alpha = norm_now / product
    direction, direction_pad, along = (resid, resid_pad, image)
    for step in range(ITERS):
        iterate = iterate + alpha * direction
        resid = resid - alpha * along
        if step + 1 < ITERS:
            resid_pad = faces(resid)
            image = operate(resid_pad, coeffs)
            norm_next, product = paired_sums(resid, image)
            ratio = norm_next / norm_now
            alpha = norm_next / (product - ratio * norm_next / alpha)
            direction = resid + ratio * direction
            along = image + ratio * along
            norm_now = norm_next
    return (iterate, iterate_pad)


def per_device(conduct, seeds, labels, start, cotangent):
    cond_pad = with_halo(conduct, (("gy", 0), ("gz", 1)), 1)
    start_pad = faces(start)
    coeffs = coefficients(cond_pad, seeds)
    rhs = seed_pull * (seeds * labels).astype(jnp.float32)
    first_resid = rhs - operate(start_pad, coeffs)
    probability, prob_pad = conjugate(start, start_pad, first_resid, coeffs)
    adjoint, adj_pad = conjugate(
        jnp.zeros_like(cotangent), jnp.zeros_like(start_pad), cotangent, coeffs
    )
    paired = with_halo(jnp.stack([probability, adjoint]), (("gy", 1), ("gz", 2)), 1)
    prob_pad = paired[0]
    adj_pad = paired[1]
    grad_conduct = gradient(cond_pad, prob_pad, adj_pad)
    return (probability, adjoint, grad_conduct)


def solution(mesh):
    in_specs = (
        P("gy", "gz", None),
        P("gy", "gz", None),
        P("gy", "gz", None),
        P("gy", "gz", None),
        P("gy", "gz", None),
    )
    out_specs = (P("gy", "gz", None), P("gy", "gz", None), P("gy", "gz", None))
    return jax.shard_map(
        per_device, mesh=mesh, in_specs=in_specs, out_specs=out_specs, check_vma=False
    )
```

profile of v0, /device:TPU:3, one launch (start us, length us, event | category | flops | bytes accessed | tf_op | source)
XLA Modules:
  0.0 203.1 jit_solution(3476084306509242845)
XLA Ops:
  3.3 4.3 %collective-permute-start.5 = (f32[1,32,128]{2,1,0:T(8,128)S(1)}, f32[1,32,128]{2,1,0:T(8,128)S(1)}, u32[]{:S(2)}, u32[]{:S(2)}) collective-permute-start(f32[1,32,128]{2,1,0:T(8,128)S(1)} %get-tuple-element.50), channel_id=1, source_target_pairs={{0,8},{8,16},{16,24},{1,9},{9,17},{17,25},{2,10},{10,18},{18,26},{... | collective-permute-start | bytes 49160 | tf_op jit(solution)/shard_map/ppermute | solution.py:16
  8.3 2.2 %collective-permute-start.1 = (f32[1,32,128]{2,1,0:T(8,128)S(1)}, f32[1,32,128]{2,1,0:T(8,128)S(1)}, u32[]{:S(2)}, u32[]{:S(2)}) collective-permute-start(f32[1,32,128]{2,1,0:T(8,128)S(1)} %get-tuple-element.52), channel_id=1, source_target_pairs={{0,8},{8,16},{16,24},{1,9},{9,17},{17,25},{2,10},{10,18},{18,26},{... | collective-permute-start | bytes 49160 | tf_op jit(solution)/shard_map/ppermute | solution.py:16
  11.2 3.0 %collective-permute-start.16 = (f32[1,32,128]{2,1,0:T(8,128)S(1)}, f32[1,32,128]{2,1,0:T(8,128)S(1)}, u32[]{:S(2)}, u32[]{:S(2)}) collective-permute-start(f32[1,32,128]{2,1,0:T(8,128)S(1)} %get-tuple-element.53), channel_id=1, source_target_pairs={{8,0},{16,8},{24,16},{9,1},{17,9},{25,17},{10,2},{18,10},{26,18},{... | collective-permute-start | bytes 49160 | tf_op jit(solution)/shard_map/ppermute | solution.py:19
  14.3 3.1 %collective-permute-start.17 = (f32[1,32,128]{2,1,0:T(8,128)S(1)}, f32[1,32,128]{2,1,0:T(8,128)S(1)}, u32[]{:S(2)}, u32[]{:S(2)}) collective-permute-start(f32[1,32,128]{2,1,0:T(8,128)S(1)} %get-tuple-element.54), channel_id=1, source_target_pairs={{0,8},{8,16},{16,24},{1,9},{9,17},{17,25},{2,10},{10,18},{18,26},{... | collective-permute-start | bytes 49160 | tf_op jit(solution)/shard_map/ppermute | solution.py:16
  17.4 2.2 %collective-permute-start = (f32[1,32,128]{2,1,0:T(8,128)S(1)}, f32[1,32,128]{2,1,0:T(8,128)S(1)}, u32[]{:S(2)}, u32[]{:S(2)}) collective-permute-start(f32[1,32,128]{2,1,0:T(8,128)S(1)} %get-tuple-element.51), channel_id=1, source_target_pairs={{8,0},{16,8},{24,16},{9,1},{17,9},{25,17},{10,2},{18,10},{26,18},{... | collective-permute-start | bytes 49160 | tf_op jit(solution)/shard_map/ppermute | solution.py:19
  20.7 2.2 %collective-permute-done = f32[1,32,128]{2,1,0:T(8,128)S(1)} collective-permute-done((f32[1,32,128]{2,1,0:T(8,128)S(1)}, f32[1,32,128]{2,1,0:T(8,128)S(1)}, u32[]{:S(2)}, u32[]{:S(2)}) %collective-permute-start) | collective-permute-done | bytes 16416 | tf_op jit(solution)/shard_map/ppermute | solution.py:19
  22.8 6.3 %collective-permute-start.3 = (f32[18,1,128]{2,1,0:T(1,128)S(1)}, f32[18,1,128]{2,1,0:T(1,128)S(1)}, u32[]{:S(2)}, u32[]{:S(2)}) collective-permute-start(f32[18,1,128]{2,1,0:T(1,128)S(1)} %get-tuple-element.39), channel_id=1, source_target_pairs={{0,1},{1,2},{2,3},{3,4},{4,5},{5,6},{6,7},{8,9},{9,10},{10,11},{11... | collective-permute-start | bytes 27656 | tf_op jit(solution)/shard_map/ppermute | solution.py:16
  29.2 1.9 collective-permute-start.2
  31.2 1.9 collective-permute-start.18
  33.2 3.6 %collective-permute-start.19 = (f32[18,1,128]{2,1,0:T(1,128)S(1)}, f32[18,1,128]{2,1,0:T(1,128)S(1)}, u32[]{:S(2)}, u32[]{:S(2)}) collective-permute-start(f32[18,1,128]{2,1,0:T(1,128)S(1)} %get-tuple-element.42), channel_id=1, source_target_pairs={{0,1},{1,2},{2,3},{3,4},{4,5},{5,6},{6,7},{8,9},{9,10},{10,11},{11... | collective-permute-start | bytes 27656 | tf_op jit(solution)/shard_map/ppermute | solution.py:16
  36.9 2.1 %collective-permute-start.6 = (f32[18,1,128]{2,1,0:T(1,128)S(1)}, f32[18,1,128]{2,1,0:T(1,128)S(1)}, u32[]{:S(2)}, u32[]{:S(2)}) collective-permute-start(f32[18,1,128]{2,1,0:T(1,128)S(1)} %get-tuple-element.37), channel_id=1, source_target_pairs={{1,0},{2,1},{3,2},{4,3},{5,4},{6,5},{7,6},{9,8},{10,9},{11,10},{12... | collective-permute-start | bytes 27656 | tf_op jit(solution)/shard_map/ppermute | solution.py:19
  39.0 3.8 %collective-permute-start.7 = (f32[18,1,128]{2,1,0:T(1,128)S(1)}, f32[18,1,128]{2,1,0:T(1,128)S(1)}, u32[]{:S(2)}, u32[]{:S(2)}) collective-permute-start(f32[18,1,128]{2,1,0:T(1,128)S(1)} %get-tuple-element.38), channel_id=1, source_target_pairs={{0,1},{1,2},{2,3},{3,4},{4,5},{5,6},{6,7},{8,9},{9,10},{10,11},{11... | collective-permute-start | bytes 27656 | tf_op jit(solution)/shard_map/ppermute | solution.py:16
  44.5 1.9 collective-permute-start.9
  46.4 3.4 %collective-permute-start.8 = (f32[1,32,128]{2,1,0:T(8,128)S(1)}, f32[1,32,128]{2,1,0:T(8,128)S(1)}, u32[]{:S(2)}, u32[]{:S(2)}) collective-permute-start(f32[1,32,128]{2,1,0:T(8,128)S(1)} %get-tuple-element.48), channel_id=1, source_target_pairs={{8,0},{16,8},{24,16},{9,1},{17,9},{25,17},{10,2},{18,10},{26,18},{... | collective-permute-start | bytes 49160 | tf_op jit(solution)/shard_map/ppermute | solution.py:19
  49.8 2.0 collective-permute-done.8
  51.8 1.9 collective-permute-start.10
  53.8 4.8 %collective-permute-start.11 = (f32[18,1,128]{2,1,0:T(1,128)S(1)}, f32[18,1,128]{2,1,0:T(1,128)S(1)}, u32[]{:S(2)}, u32[]{:S(2)}) collective-permute-start(f32[18,1,128]{2,1,0:T(1,128)S(1)} %get-tuple-element.36), channel_id=1, source_target_pairs={{0,1},{1,2},{2,3},{3,4},{4,5},{5,6},{6,7},{8,9},{9,10},{10,11},{11... | collective-permute-start | bytes 27656 | tf_op jit(solution)/shard_map/ppermute | solution.py:16
  60.4 40.6 %all-reduce.9 = (f32[]{:T(128)}, f32[]{:T(128)}, f32[]{:T(128)}, f32[]{:T(128)}) all-reduce(f32[]{:T(128)} %get-tuple-element.6, f32[]{:T(128)} %get-tuple-element.5, f32[]{:T(128)} %get-tuple-element.4, f32[]{:T(128)} %get-tuple-element.3), channel_id=1, replica_groups=mesh['gy'=4,'gz'=8] {'gy','gz'}, use_global_device_ids=true, to_apply=%region_1.2 | all-reduce | flops 4 | bytes 32 | tf_op jit(solution)/shard_map/psum | solution.py:77
  103.6 3.1 %collective-permute-start.21 = (f32[1,32,128]{2,1,0:T(8,128)}, f32[1,32,128]{2,1,0:T(8,128)S(1)}, u32[]{:S(2)}, u32[]{:S(2)}) collective-permute-start(f32[1,32,128]{2,1,0:T(8,128)} %get-tuple-element.43), channel_id=1, source_target_pairs={{0,8},{8,16},{16,24},{1,9},{9,17},{17,25},{2,10},{10,18},{18,26},{... | collective-permute-start | bytes 49160 | tf_op jit(solution)/shard_map/ppermute | solution.py:16
  106.7 2.2 %collective-permute-start.20 = (f32[1,32,128]{2,1,0:T(8,128)S(1)}, f32[1,32,128]{2,1,0:T(8,128)S(1)}, u32[]{:S(2)}, u32[]{:S(2)}) collective-permute-start(f32[1,32,128]{2,1,0:T(8,128)S(1)} %get-tuple-element.44), channel_id=1, source_target_pairs={{8,0},{16,8},{24,16},{9,1},{17,9},{25,17},{10,2},{18,10},{26,18},{... | collective-permute-start | bytes 49160 | tf_op jit(solution)/shard_map/ppermute | solution.py:19
  111.0 4.0 %collective-permute-start.13 = (f32[1,32,128]{2,1,0:T(8,128)S(1)}, f32[1,32,128]{2,1,0:T(8,128)S(1)}, u32[]{:S(2)}, u32[]{:S(2)}) collective-permute-start(f32[1,32,128]{2,1,0:T(8,128)S(1)} %get-tuple-element.45), channel_id=1, source_target_pairs={{0,8},{8,16},{16,24},{1,9},{9,17},{17,25},{2,10},{10,18},{18,26},{... | collective-permute-start | bytes 49160 | tf_op jit(solution)/shard_map/ppermute | solution.py:16
  115.0 1.9 collective-permute-start.12
  116.9 4.8 %collective-permute-start.22 = (f32[18,1,128]{2,1,0:T(1,128)S(1)}, f32[18,1,128]{2,1,0:T(1,128)S(1)}, u32[]{:S(2)}, u32[]{:S(2)}) collective-permute-start(f32[18,1,128]{2,1,0:T(1,128)S(1)} %get-tuple-element.31), channel_id=1, source_target_pairs={{1,0},{2,1},{3,2},{4,3},{5,4},{6,5},{7,6},{9,8},{10,9},{11,10},{12... | collective-permute-start | bytes 27656 | tf_op jit(solution)/shard_map/ppermute | solution.py:19
  121.7 3.0 %collective-permute-start.23 = (f32[18,1,128]{2,1,0:T(1,128)S(1)}, f32[18,1,128]{2,1,0:T(1,128)S(1)}, u32[]{:S(2)}, u32[]{:S(2)}) collective-permute-start(f32[18,1,128]{2,1,0:T(1,128)S(1)} %get-tuple-element.32), channel_id=1, source_target_pairs={{0,1},{1,2},{2,3},{3,4},{4,5},{5,6},{6,7},{8,9},{9,10},{10,11},{11... | collective-permute-start | bytes 27656 | tf_op jit(solution)/shard_map/ppermute | solution.py:16
  124.8 1.9 collective-permute-start.14
  126.7 3.6 %collective-permute-start.15 = (f32[18,1,128]{2,1,0:T(1,128)S(1)}, f32[18,1,128]{2,1,0:T(1,128)S(1)}, u32[]{:S(2)}, u32[]{:S(2)}) collective-permute-start(f32[18,1,128]{2,1,0:T(1,128)S(1)} %get-tuple-element.34), channel_id=1, source_target_pairs={{0,1},{1,2},{2,3},{3,4},{4,5},{5,6},{6,7},{8,9},{9,10},{10,11},{11... | collective-permute-start | bytes 27656 | tf_op jit(solution)/shard_map/ppermute | solution.py:16
  132.4 41.4 %all-reduce.8 = (f32[]{:T(128)}, f32[]{:T(128)}, f32[]{:T(128)}, f32[]{:T(128)}) all-reduce(f32[]{:T(128)} %get-tuple-element.17, f32[]{:T(128)} %fusion.36, f32[]{:T(128)} %get-tuple-element.15, f32[]{:T(128)} %fusion.46), channel_id=1, replica_groups=mesh['gy'=4,'gz'=8] {'gy','gz'}, use_global_device_ids=true, to_apply=%region_5.6 | all-reduce | flops 4 | bytes 32 | tf_op jit(solution)/shard_map/psum | solution.py:77
  183.2 3.1 %collective-permute-start.24 = (f32[2,1,32,128]{3,2,1,0:T(8,128)S(1)}, f32[2,1,32,128]{3,2,1,0:T(8,128)S(1)}, u32[]{:S(2)}, u32[]{:S(2)}) collective-permute-start(f32[2,1,32,128]{3,2,1,0:T(8,128)S(1)} %get-tuple-element.29), channel_id=1, source_target_pairs={{0,8},{8,16},{16,24},{1,9},{9,17},{17,25},{2,10},{10,18},{18,26},{... | collective-permute-start | bytes 98312 | tf_op jit(solution)/shard_map/ppermute | solution.py:16
  186.4 2.2 %collective-permute-start.25 = (f32[2,1,32,128]{3,2,1,0:T(8,128)S(1)}, f32[2,1,32,128]{3,2,1,0:T(8,128)S(1)}, u32[]{:S(2)}, u32[]{:S(2)}) collective-permute-start(f32[2,1,32,128]{3,2,1,0:T(8,128)S(1)} %get-tuple-element.30), channel_id=1, source_target_pairs={{8,0},{16,8},{24,16},{9,1},{17,9},{25,17},{10,2},{18,10},{26,18},{... | collective-permute-start | bytes 98312 | tf_op jit(solution)/shard_map/ppermute | solution.py:19
  188.6 3.4 %collective-permute-done.25 = f32[2,1,32,128]{3,2,1,0:T(8,128)S(1)} collective-permute-done((f32[2,1,32,128]{3,2,1,0:T(8,128)S(1)}, f32[2,1,32,128]{3,2,1,0:T(8,128)S(1)}, u32[]{:S(2)}, u32[]{:S(2)}) %collective-permute-start.25) | collective-permute-done | bytes 32800 | tf_op jit(solution)/shard_map/ppermute | solution.py:19
  191.9 4.4 %collective-permute-start.26 = (f32[2,18,1,128]{3,2,1,0:T(1,128)S(1)}, f32[2,18,1,128]{3,2,1,0:T(1,128)S(1)}, u32[]{:S(2)}, u32[]{:S(2)}) collective-permute-start(f32[2,18,1,128]{3,2,1,0:T(1,128)S(1)} %get-tuple-element.27), channel_id=1, source_target_pairs={{0,1},{1,2},{2,3},{3,4},{4,5},{5,6},{6,7},{8,9},{9,10},{10,11},{11... | collective-permute-start | bytes 55304 | tf_op jit(solution)/shard_map/ppermute | solution.py:16
  198.3 3.1 %collective-permute-done.27 = f32[2,18,1,128]{3,2,1,0:T(1,128)S(1)} collective-permute-done((f32[2,18,1,128]{3,2,1,0:T(1,128)S(1)}, f32[2,18,1,128]{3,2,1,0:T(1,128)S(1)}, u32[]{:S(2)}, u32[]{:S(2)}) %collective-permute-start.27) | collective-permute-done | bytes 18464 | tf_op jit(solution)/shard_map/ppermute | solution.py:19
  (76 shorter events, 16.6 us)
Async XLA Ops:
  1.4 35.5 %collective-permute-start.4 = (f32[1,32,128]{2,1,0:T(8,128)S(1)}, f32[1,32,128]{2,1,0:T(8,128)S(1)}, u32[]{:S(2)}, u32[]{:S(2)}) collective-permute-start(f32[1,32,128]{2,1,0:T(8,128)S(1)} %get-tuple-element.49), channel_id=1, source_target_pairs={{8,0},{16,8},{24,16},{9,1},{17,9},{25,17},{10,2},{18,10},{26,18},{... | collective-permute-start | bytes 49160 | tf_op jit(solution)/shard_map/ppermute | solution.py:19
  3.3 29.9 %collective-permute-start.5 = (f32[1,32,128]{2,1,0:T(8,128)S(1)}, f32[1,32,128]{2,1,0:T(8,128)S(1)}, u32[]{:S(2)}, u32[]{:S(2)}) collective-permute-start(f32[1,32,128]{2,1,0:T(8,128)S(1)} %get-tuple-element.50), channel_id=1, source_target_pairs={{0,8},{8,16},{16,24},{1,9},{9,17},{17,25},{2,10},{10,18},{18,26},{... | collective-permute-start | bytes 49160 | tf_op jit(solution)/shard_map/ppermute | solution.py:16
  8.3 9.1 %collective-permute-start.1 = (f32[1,32,128]{2,1,0:T(8,128)S(1)}, f32[1,32,128]{2,1,0:T(8,128)S(1)}, u32[]{:S(2)}, u32[]{:S(2)}) collective-permute-start(f32[1,32,128]{2,1,0:T(8,128)S(1)} %get-tuple-element.52), channel_id=1, source_target_pairs={{0,8},{8,16},{16,24},{1,9},{9,17},{17,25},{2,10},{10,18},{18,26},{... | collective-permute-start | bytes 49160 | tf_op jit(solution)/shard_map/ppermute | solution.py:16
  11.2 19.9 %collective-permute-start.16 = (f32[1,32,128]{2,1,0:T(8,128)S(1)}, f32[1,32,128]{2,1,0:T(8,128)S(1)}, u32[]{:S(2)}, u32[]{:S(2)}) collective-permute-start(f32[1,32,128]{2,1,0:T(8,128)S(1)} %get-tuple-element.53), channel_id=1, source_target_pairs={{8,0},{16,8},{24,16},{9,1},{17,9},{25,17},{10,2},{18,10},{26,18},{... | collective-permute-start | bytes 49160 | tf_op jit(solution)/shard_map/ppermute | solution.py:19
  14.3 14.9 %collective-permute-start.17 = (f32[1,32,128]{2,1,0:T(8,128)S(1)}, f32[1,32,128]{2,1,0:T(8,128)S(1)}, u32[]{:S(2)}, u32[]{:S(2)}) collective-permute-start(f32[1,32,128]{2,1,0:T(8,128)S(1)} %get-tuple-element.54), channel_id=1, source_target_pairs={{0,8},{8,16},{16,24},{1,9},{9,17},{17,25},{2,10},{10,18},{18,26},{... | collective-permute-start | bytes 49160 | tf_op jit(solution)/shard_map/ppermute | solution.py:16
  17.4 5.4 %collective-permute-start = (f32[1,32,128]{2,1,0:T(8,128)S(1)}, f32[1,32,128]{2,1,0:T(8,128)S(1)}, u32[]{:S(2)}, u32[]{:S(2)}) collective-permute-start(f32[1,32,128]{2,1,0:T(8,128)S(1)} %get-tuple-element.51), channel_id=1, source_target_pairs={{8,0},{16,8},{24,16},{9,1},{17,9},{25,17},{10,2},{18,10},{26,18},{... | collective-permute-start | bytes 49160 | tf_op jit(solution)/shard_map/ppermute | solution.py:19
  19.6 11.5 %copy-start.2 = (f32[16,32,128]{2,1,0:T(8,128)S(1)}, f32[16,32,128]{2,1,0:T(8,128)}, u32[]{:S(2)}) copy-start(f32[16,32,128]{2,1,0:T(8,128)} %param.9) | copy-start | bytes 786436
  22.8 16.1 %collective-permute-start.3 = (f32[18,1,128]{2,1,0:T(1,128)S(1)}, f32[18,1,128]{2,1,0:T(1,128)S(1)}, u32[]{:S(2)}, u32[]{:S(2)}) collective-permute-start(f32[18,1,128]{2,1,0:T(1,128)S(1)} %get-tuple-element.39), channel_id=1, source_target_pairs={{0,1},{1,2},{2,3},{3,4},{4,5},{5,6},{6,7},{8,9},{9,10},{10,11},{11... | collective-permute-start | bytes 27656 | tf_op jit(solution)/shard_map/ppermute | solution.py:16
  29.2 13.6 %collective-permute-start.2 = (f32[18,1,128]{2,1,0:T(1,128)S(1)}, f32[18,1,128]{2,1,0:T(1,128)S(1)}, u32[]{:S(2)}, u32[]{:S(2)}) collective-permute-start(f32[18,1,128]{2,1,0:T(1,128)S(1)} %get-tuple-element.40), channel_id=1, source_target_pairs={{1,0},{2,1},{3,2},{4,3},{5,4},{6,5},{7,6},{9,8},{10,9},{11,10},{12... | collective-permute-start | bytes 27656 | tf_op jit(solution)/shard_map/ppermute | solution.py:19
  31.2 11.6 %collective-permute-start.18 = (f32[18,1,128]{2,1,0:T(1,128)S(1)}, f32[18,1,128]{2,1,0:T(1,128)S(1)}, u32[]{:S(2)}, u32[]{:S(2)}) collective-permute-start(f32[18,1,128]{2,1,0:T(1,128)S(1)} %get-tuple-element.41), channel_id=1, source_target_pairs={{1,0},{2,1},{3,2},{4,3},{5,4},{6,5},{7,6},{9,8},{10,9},{11,10},{12... | collective-permute-start | bytes 27656 | tf_op jit(solution)/shard_map/ppermute | solution.py:19
  33.2 9.7 %collective-permute-start.19 = (f32[18,1,128]{2,1,0:T(1,128)S(1)}, f32[18,1,128]{2,1,0:T(1,128)S(1)}, u32[]{:S(2)}, u32[]{:S(2)}) collective-permute-start(f32[18,1,128]{2,1,0:T(1,128)S(1)} %get-tuple-element.42), channel_id=1, source_target_pairs={{0,1},{1,2},{2,3},{3,4},{4,5},{5,6},{6,7},{8,9},{9,10},{10,11},{11... | collective-permute-start | bytes 27656 | tf_op jit(solution)/shard_map/ppermute | solution.py:16
  36.8 6.0 %copy-start = (f32[16,32,128]{2,1,0:T(8,128)S(1)}, f32[16,32,128]{2,1,0:T(8,128)}, u32[]{:S(2)}) copy-start(f32[16,32,128]{2,1,0:T(8,128)} %param.5) | copy-start | bytes 786436
  36.9 7.2 %collective-permute-start.6 = (f32[18,1,128]{2,1,0:T(1,128)S(1)}, f32[18,1,128]{2,1,0:T(1,128)S(1)}, u32[]{:S(2)}, u32[]{:S(2)}) collective-permute-start(f32[18,1,128]{2,1,0:T(1,128)S(1)} %get-tuple-element.37), channel_id=1, source_target_pairs={{1,0},{2,1},{3,2},{4,3},{5,4},{6,5},{7,6},{9,8},{10,9},{11,10},{12... | collective-permute-start | bytes 27656 | tf_op jit(solution)/shard_map/ppermute | solution.py:19
  39.0 5.1 %collective-permute-start.7 = (f32[18,1,128]{2,1,0:T(1,128)S(1)}, f32[18,1,128]{2,1,0:T(1,128)S(1)}, u32[]{:S(2)}, u32[]{:S(2)}) collective-permute-start(f32[18,1,128]{2,1,0:T(1,128)S(1)} %get-tuple-element.38), channel_id=1, source_target_pairs={{0,1},{1,2},{2,3},{3,4},{4,5},{5,6},{6,7},{8,9},{9,10},{10,11},{11... | collective-permute-start | bytes 27656 | tf_op jit(solution)/shard_map/ppermute | solution.py:16
  44.5 5.3 %collective-permute-start.9 = (f32[1,32,128]{2,1,0:T(8,128)S(1)}, f32[1,32,128]{2,1,0:T(8,128)S(1)}, u32[]{:S(2)}, u32[]{:S(2)}) collective-permute-start(f32[1,32,128]{2,1,0:T(8,128)S(1)} %get-tuple-element.47), channel_id=1, source_target_pairs={{0,8},{8,16},{16,24},{1,9},{9,17},{17,25},{2,10},{10,18},{18,26},{... | collective-permute-start | bytes 49160 | tf_op jit(solution)/shard_map/ppermute | solution.py:16
  46.4 5.4 %collective-permute-start.8 = (f32[1,32,128]{2,1,0:T(8,128)S(1)}, f32[1,32,128]{2,1,0:T(8,128)S(1)}, u32[]{:S(2)}, u32[]{:S(2)}) collective-permute-start(f32[1,32,128]{2,1,0:T(8,128)S(1)} %get-tuple-element.48), channel_id=1, source_target_pairs={{8,0},{16,8},{24,16},{9,1},{17,9},{25,17},{10,2},{18,10},{26,18},{... | collective-permute-start | bytes 49160 | tf_op jit(solution)/shard_map/ppermute | solution.py:19
  51.8 6.8 %collective-permute-start.10 = (f32[18,1,128]{2,1,0:T(1,128)S(1)}, f32[18,1,128]{2,1,0:T(1,128)S(1)}, u32[]{:S(2)}, u32[]{:S(2)}) collective-permute-start(f32[18,1,128]{2,1,0:T(1,128)S(1)} %get-tuple-element.35), channel_id=1, source_target_pairs={{1,0},{2,1},{3,2},{4,3},{5,4},{6,5},{7,6},{9,8},{10,9},{11,10},{12... | collective-permute-start | bytes 27656 | tf_op jit(solution)/shard_map/ppermute | solution.py:19
  53.8 5.6 %collective-permute-start.11 = (f32[18,1,128]{2,1,0:T(1,128)S(1)}, f32[18,1,128]{2,1,0:T(1,128)S(1)}, u32[]{:S(2)}, u32[]{:S(2)}) collective-permute-start(f32[18,1,128]{2,1,0:T(1,128)S(1)} %get-tuple-element.36), channel_id=1, source_target_pairs={{0,1},{1,2},{2,3},{3,4},{4,5},{5,6},{6,7},{8,9},{9,10},{10,11},{11... | collective-permute-start | bytes 27656 | tf_op jit(solution)/shard_map/ppermute | solution.py:16
  103.6 13.3 %collective-permute-start.21 = (f32[1,32,128]{2,1,0:T(8,128)}, f32[1,32,128]{2,1,0:T(8,128)S(1)}, u32[]{:S(2)}, u32[]{:S(2)}) collective-permute-start(f32[1,32,128]{2,1,0:T(8,128)} %get-tuple-element.43), channel_id=1, source_target_pairs={{0,8},{8,16},{16,24},{1,9},{9,17},{17,25},{2,10},{10,18},{18,26},{... | collective-permute-start | bytes 49160 | tf_op jit(solution)/shard_map/ppermute | solution.py:16
  106.7 10.2 %collective-permute-start.20 = (f32[1,32,128]{2,1,0:T(8,128)S(1)}, f32[1,32,128]{2,1,0:T(8,128)S(1)}, u32[]{:S(2)}, u32[]{:S(2)}) collective-permute-start(f32[1,32,128]{2,1,0:T(8,128)S(1)} %get-tuple-element.44), channel_id=1, source_target_pairs={{8,0},{16,8},{24,16},{9,1},{17,9},{25,17},{10,2},{18,10},{26,18},{... | collective-permute-start | bytes 49160 | tf_op jit(solution)/shard_map/ppermute | solution.py:19
  111.0 13.8 %collective-permute-start.13 = (f32[1,32,128]{2,1,0:T(8,128)S(1)}, f32[1,32,128]{2,1,0:T(8,128)S(1)}, u32[]{:S(2)}, u32[]{:S(2)}) collective-permute-start(f32[1,32,128]{2,1,0:T(8,128)S(1)} %get-tuple-element.45), channel_id=1, source_target_pairs={{0,8},{8,16},{16,24},{1,9},{9,17},{17,25},{2,10},{10,18},{18,26},{... | collective-permute-start | bytes 49160 | tf_op jit(solution)/shard_map/ppermute | solution.py:16
  115.0 9.8 %collective-permute-start.12 = (f32[1,32,128]{2,1,0:T(8,128)S(1)}, f32[1,32,128]{2,1,0:T(8,128)S(1)}, u32[]{:S(2)}, u32[]{:S(2)}) collective-permute-start(f32[1,32,128]{2,1,0:T(8,128)S(1)} %get-tuple-element.46), channel_id=1, source_target_pairs={{8,0},{16,8},{24,16},{9,1},{17,9},{25,17},{10,2},{18,10},{26,18},{... | collective-permute-start | bytes 49160 | tf_op jit(solution)/shard_map/ppermute | solution.py:19
  116.9 13.4 %collective-permute-start.22 = (f32[18,1,128]{2,1,0:T(1,128)S(1)}, f32[18,1,128]{2,1,0:T(1,128)S(1)}, u32[]{:S(2)}, u32[]{:S(2)}) collective-permute-start(f32[18,1,128]{2,1,0:T(1,128)S(1)} %get-tuple-element.31), channel_id=1, source_target_pairs={{1,0},{2,1},{3,2},{4,3},{5,4},{6,5},{7,6},{9,8},{10,9},{11,10},{12... | collective-permute-start | bytes 27656 | tf_op jit(solution)/shard_map/ppermute | solution.py:19
  121.7 8.7 %collective-permute-start.23 = (f32[18,1,128]{2,1,0:T(1,128)S(1)}, f32[18,1,128]{2,1,0:T(1,128)S(1)}, u32[]{:S(2)}, u32[]{:S(2)}) collective-permute-start(f32[18,1,128]{2,1,0:T(1,128)S(1)} %get-tuple-element.32), channel_id=1, source_target_pairs={{0,1},{1,2},{2,3},{3,4},{4,5},{5,6},{6,7},{8,9},{9,10},{10,11},{11... | collective-permute-start | bytes 27656 | tf_op jit(solution)/shard_map/ppermute | solution.py:16
  124.8 6.6 %collective-permute-start.14 = (f32[18,1,128]{2,1,0:T(1,128)S(1)}, f32[18,1,128]{2,1,0:T(1,128)S(1)}, u32[]{:S(2)}, u32[]{:S(2)}) collective-permute-start(f32[18,1,128]{2,1,0:T(1,128)S(1)} %get-tuple-element.33), channel_id=1, source_target_pairs={{1,0},{2,1},{3,2},{4,3},{5,4},{6,5},{7,6},{9,8},{10,9},{11,10},{12... | collective-permute-start | bytes 27656 | tf_op jit(solution)/shard_map/ppermute | solution.py:19
  126.7 4.7 %collective-permute-start.15 = (f32[18,1,128]{2,1,0:T(1,128)S(1)}, f32[18,1,128]{2,1,0:T(1,128)S(1)}, u32[]{:S(2)}, u32[]{:S(2)}) collective-permute-start(f32[18,1,128]{2,1,0:T(1,128)S(1)} %get-tuple-element.34), channel_id=1, source_target_pairs={{0,1},{1,2},{2,3},{3,4},{4,5},{5,6},{6,7},{8,9},{9,10},{10,11},{11... | collective-permute-start | bytes 27656 | tf_op jit(solution)/shard_map/ppermute | solution.py:16
  183.2 18.2 %copy-start.3 = (f32[16,32,128]{2,1,0:T(8,128)}, f32[16,32,128]{2,1,0:T(8,128)S(1)}, u32[]{:S(2)}) copy-start(f32[16,32,128]{2,1,0:T(8,128)S(1)} %get-tuple-element.55) | copy-start | bytes 786436
  183.2 18.2 %copy-start.4 = (f32[16,32,128]{2,1,0:T(8,128)}, f32[16,32,128]{2,1,0:T(8,128)S(1)}, u32[]{:S(2)}) copy-start(f32[16,32,128]{2,1,0:T(8,128)S(1)} %get-tuple-element.56) | copy-start | bytes 786436
  183.2 5.3 %collective-permute-start.24 = (f32[2,1,32,128]{3,2,1,0:T(8,128)S(1)}, f32[2,1,32,128]{3,2,1,0:T(8,128)S(1)}, u32[]{:S(2)}, u32[]{:S(2)}) collective-permute-start(f32[2,1,32,128]{3,2,1,0:T(8,128)S(1)} %get-tuple-element.29), channel_id=1, source_target_pairs={{0,8},{8,16},{16,24},{1,9},{9,17},{17,25},{2,10},{10,18},{18,26},{... | collective-permute-start | bytes 98312 | tf_op jit(solution)/shard_map/ppermute | solution.py:16
  186.4 5.6 %collective-permute-start.25 = (f32[2,1,32,128]{3,2,1,0:T(8,128)S(1)}, f32[2,1,32,128]{3,2,1,0:T(8,128)S(1)}, u32[]{:S(2)}, u32[]{:S(2)}) collective-permute-start(f32[2,1,32,128]{3,2,1,0:T(8,128)S(1)} %get-tuple-element.30), channel_id=1, source_target_pairs={{8,0},{16,8},{24,16},{9,1},{17,9},{25,17},{10,2},{18,10},{26,18},{... | collective-permute-start | bytes 98312 | tf_op jit(solution)/shard_map/ppermute | solution.py:19
  191.9 6.3 %collective-permute-start.26 = (f32[2,18,1,128]{3,2,1,0:T(1,128)S(1)}, f32[2,18,1,128]{3,2,1,0:T(1,128)S(1)}, u32[]{:S(2)}, u32[]{:S(2)}) collective-permute-start(f32[2,18,1,128]{3,2,1,0:T(1,128)S(1)} %get-tuple-element.27), channel_id=1, source_target_pairs={{0,1},{1,2},{2,3},{3,4},{4,5},{5,6},{6,7},{8,9},{9,10},{10,11},{11... | collective-permute-start | bytes 55304 | tf_op jit(solution)/shard_map/ppermute | solution.py:16
  196.4 5.1 %collective-permute-start.27 = (f32[2,18,1,128]{3,2,1,0:T(1,128)S(1)}, f32[2,18,1,128]{3,2,1,0:T(1,128)S(1)}, u32[]{:S(2)}, u32[]{:S(2)}) collective-permute-start(f32[2,18,1,128]{3,2,1,0:T(1,128)S(1)} %get-tuple-element.28), channel_id=1, source_target_pairs={{1,0},{2,1},{3,2},{4,3},{5,4},{6,5},{7,6},{9,8},{10,9},{11,10},{12... | collective-permute-start | bytes 55304 | tf_op jit(solution)/shard_map/ppermute | solution.py:19
  (3 other events, 16.8 us)
where the time goes:
time: 205 us; the launch traced here: 203 us
  starting transfers between devices  84.5 us (41%)
  blocking collectives  82 us (40%)
  between operations  13.2 us (6%)
  waiting for transfers between devices  11.5 us (6%)
  other arithmetic  7.82 us (4%)
  local copies, waits for them, and re-layouts  4.1 us (2%)
    psum x2, blocking collectives, paired_sums(): lax.psum((jnp.sum(resid * resid), jnp.sum(resid * image)), ('gy', 'gz'))  82 us
    ppermute x14, starting transfers between devices, with_halo(): lax.ppermute(lax.slice_in_dim(block, block.shape[dim] - width, None, axis...  51.3 us
    ppermute x14, starting transfers between devices, with_halo(): lax.ppermute(lax.slice_in_dim(block, 0, width, axis=dim), axis, backward)  33.2 us
    ppermute x14, waiting for transfers between devices, with_halo(): lax.ppermute(lax.slice_in_dim(block, 0, width, axis=dim), axis, backward)  10.7 us
    reduce_sum x4, other arithmetic, paired_sums(): jnp.sum(resid * image)  4.26 us
  transfers between devices with their start and end apart: 28, of which 5 were waited for; matrix products, arithmetic and copies ran while one was open for 3% of the time, Pallas kernels for 0%

commit v1 on v0

--- a/solution.py
+++ b/solution.py
@@ -6,6 +6,7 @@
 ITERS = 2
 seed_pull = 4.0
 screening = 0.05
+return_all_clusters_up = lambda arr_in: lax.psum(lax.psum(arr_in, axis_name="gz"), axis_name="gy")
 
 
 def with_halo(block, sides, width):
@@ -74,7 +75,7 @@
 
 
 def paired_sums(resid, image):
-    return lax.psum((jnp.sum(resid * resid), jnp.sum(resid * image)), ("gy", "gz"))
+    return return_all_clusters_up((jnp.sum(resid * resid), jnp.sum(resid * image)))
 
 
 def conjugate(iterate, iterate_pad, resid, coeffs):

time: 205 us -> 168 us (0.82)
  blocking collectives: 82 us -> 43.5 us
  starting transfers between devices: 84.5 us -> 87.6 us
    psum x2 -> x4, blocking collectives: 82 us -> 43.5 us  [the longest x2 28 us: lax.psum(arr_in, axis_name='gz')]
    ppermute x14, starting transfers between devices: 33.2 us -> 37.4 us  [with_halo(): lax.ppermute(lax.slice_in_dim(block, 0, width, axis=dim), axis, backward)]
where the time goes in v1:
time: 168 us; the launch traced here: 166 us
  starting transfers between devices  87.6 us (52%)
  blocking collectives  43.5 us (26%)
  between operations  13.2 us (8%)
  waiting for transfers between devices  10.1 us (6%)
  other arithmetic  7.91 us (5%)
  local copies, waits for them, and re-layouts  4.1 us (2%)
    ppermute x14, starting transfers between devices, with_halo(): lax.ppermute(lax.slice_in_dim(block, block.shape[dim] - width, None, axis...  50.2 us
    ppermute x14, starting transfers between devices, with_halo(): lax.ppermute(lax.slice_in_dim(block, 0, width, axis=dim), axis, backward)  37.4 us
    psum x2, blocking collectives, lax.psum(arr_in, axis_name='gz')  28 us
    psum x2, blocking collectives, lax.psum(lax.psum(arr_in, axis_name='gz'), axis_name='gy')  15.5 us
    ppermute x14, waiting for transfers between devices, with_halo(): lax.ppermute(lax.slice_in_dim(block, 0, width, axis=dim), axis, backward)  9.29 us
    reduce_sum x4, other arithmetic, paired_sums(): jnp.sum(resid * image)  4.26 us
  transfers between devices with their start and end apart: 28, of which 5 were waited for; matrix products, arithmetic and copies ran while one was open for 3% of the time, Pallas kernels for 0%

profile of v1, /device:TPU:3, one launch (start us, length us, event | category | flops | bytes accessed | tf_op | source)
XLA Modules:
  0.0 166.4 jit_solution(7166693965967703496)
XLA Ops:
  3.3 4.3 %collective-permute-start.5 = (f32[1,32,128]{2,1,0:T(8,128)S(1)}, f32[1,32,128]{2,1,0:T(8,128)S(1)}, u32[]{:S(2)}, u32[]{:S(2)}) collective-permute-start(f32[1,32,128]{2,1,0:T(8,128)S(1)} %get-tuple-element.58), channel_id=1, source_target_pairs={{0,8},{8,16},{16,24},{1,9},{9,17},{17,25},{2,10},{10,18},{18,26},{... | collective-permute-start | bytes 49160 | tf_op jit(solution)/shard_map/ppermute | solution.py:17
  8.3 2.2 %collective-permute-start.1 = (f32[1,32,128]{2,1,0:T(8,128)S(1)}, f32[1,32,128]{2,1,0:T(8,128)S(1)}, u32[]{:S(2)}, u32[]{:S(2)}) collective-permute-start(f32[1,32,128]{2,1,0:T(8,128)S(1)} %get-tuple-element.60), channel_id=1, source_target_pairs={{0,8},{8,16},{16,24},{1,9},{9,17},{17,25},{2,10},{10,18},{18,26},{... | collective-permute-start | bytes 49160 | tf_op jit(solution)/shard_map/ppermute | solution.py:17
  11.2 3.0 %collective-permute-start.16 = (f32[1,32,128]{2,1,0:T(8,128)S(1)}, f32[1,32,128]{2,1,0:T(8,128)S(1)}, u32[]{:S(2)}, u32[]{:S(2)}) collective-permute-start(f32[1,32,128]{2,1,0:T(8,128)S(1)} %get-tuple-element.61), channel_id=1, source_target_pairs={{8,0},{16,8},{24,16},{9,1},{17,9},{25,17},{10,2},{18,10},{26,18},{... | collective-permute-start | bytes 49160 | tf_op jit(solution)/shard_map/ppermute | solution.py:20
  14.3 3.1 %collective-permute-start.17 = (f32[1,32,128]{2,1,0:T(8,128)S(1)}, f32[1,32,128]{2,1,0:T(8,128)S(1)}, u32[]{:S(2)}, u32[]{:S(2)}) collective-permute-start(f32[1,32,128]{2,1,0:T(8,128)S(1)} %get-tuple-element.62), channel_id=1, source_target_pairs={{0,8},{8,16},{16,24},{1,9},{9,17},{17,25},{2,10},{10,18},{18,26},{... | collective-permute-start | bytes 49160 | tf_op jit(solution)/shard_map/ppermute | solution.py:17
  17.4 2.2 %collective-permute-start = (f32[1,32,128]{2,1,0:T(8,128)S(1)}, f32[1,32,128]{2,1,0:T(8,128)S(1)}, u32[]{:S(2)}, u32[]{:S(2)}) collective-permute-start(f32[1,32,128]{2,1,0:T(8,128)S(1)} %get-tuple-element.59), channel_id=1, source_target_pairs={{8,0},{16,8},{24,16},{9,1},{17,9},{25,17},{10,2},{18,10},{26,18},{... | collective-permute-start | bytes 49160 | tf_op jit(solution)/shard_map/ppermute | solution.py:20
  20.7 2.2 %collective-permute-done = f32[1,32,128]{2,1,0:T(8,128)S(1)} collective-permute-done((f32[1,32,128]{2,1,0:T(8,128)S(1)}, f32[1,32,128]{2,1,0:T(8,128)S(1)}, u32[]{:S(2)}, u32[]{:S(2)}) %collective-permute-start) | collective-permute-done | bytes 16416 | tf_op jit(solution)/shard_map/ppermute | solution.py:20
  22.8 6.3 %collective-permute-start.3 = (f32[18,1,128]{2,1,0:T(1,128)S(1)}, f32[18,1,128]{2,1,0:T(1,128)S(1)}, u32[]{:S(2)}, u32[]{:S(2)}) collective-permute-start(f32[18,1,128]{2,1,0:T(1,128)S(1)} %get-tuple-element.47), channel_id=1, source_target_pairs={{0,1},{1,2},{2,3},{3,4},{4,5},{5,6},{6,7},{8,9},{9,10},{10,11},{11... | collective-permute-start | bytes 27656 | tf_op jit(solution)/shard_map/ppermute | solution.py:17
  31.2 1.9 %collective-permute-start.18 = (f32[18,1,128]{2,1,0:T(1,128)S(1)}, f32[18,1,128]{2,1,0:T(1,128)S(1)}, u32[]{:S(2)}, u32[]{:S(2)}) collective-permute-start(f32[18,1,128]{2,1,0:T(1,128)S(1)} %get-tuple-element.49), channel_id=1, source_target_pairs={{1,0},{2,1},{3,2},{4,3},{5,4},{6,5},{7,6},{9,8},{10,9},{11,10},{12... | collective-permute-start | bytes 27656 | tf_op jit(solution)/shard_map/ppermute | solution.py:20
  33.2 3.6 %collective-permute-start.19 = (f32[18,1,128]{2,1,0:T(1,128)S(1)}, f32[18,1,128]{2,1,0:T(1,128)S(1)}, u32[]{:S(2)}, u32[]{:S(2)}) collective-permute-start(f32[18,1,128]{2,1,0:T(1,128)S(1)} %get-tuple-element.50), channel_id=1, source_target_pairs={{0,1},{1,2},{2,3},{3,4},{4,5},{5,6},{6,7},{8,9},{9,10},{10,11},{11... | collective-permute-start | bytes 27656 | tf_op jit(solution)/shard_map/ppermute | solution.py:17
  36.9 2.1 %collective-permute-start.6 = (f32[18,1,128]{2,1,0:T(1,128)S(1)}, f32[18,1,128]{2,1,0:T(1,128)S(1)}, u32[]{:S(2)}, u32[]{:S(2)}) collective-permute-start(f32[18,1,128]{2,1,0:T(1,128)S(1)} %get-tuple-element.45), channel_id=1, source_target_pairs={{1,0},{2,1},{3,2},{4,3},{5,4},{6,5},{7,6},{9,8},{10,9},{11,10},{12... | collective-permute-start | bytes 27656 | tf_op jit(solution)/shard_map/ppermute | solution.py:20
  39.0 3.8 %collective-permute-start.7 = (f32[18,1,128]{2,1,0:T(1,128)S(1)}, f32[18,1,128]{2,1,0:T(1,128)S(1)}, u32[]{:S(2)}, u32[]{:S(2)}) collective-permute-start(f32[18,1,128]{2,1,0:T(1,128)S(1)} %get-tuple-element.46), channel_id=1, source_target_pairs={{0,1},{1,2},{2,3},{3,4},{4,5},{5,6},{6,7},{8,9},{9,10},{10,11},{11... | collective-permute-start | bytes 27656 | tf_op jit(solution)/shard_map/ppermute | solution.py:17
  46.4 3.4 %collective-permute-start.8 = (f32[1,32,128]{2,1,0:T(8,128)S(1)}, f32[1,32,128]{2,1,0:T(8,128)S(1)}, u32[]{:S(2)}, u32[]{:S(2)}) collective-permute-start(f32[1,32,128]{2,1,0:T(8,128)S(1)} %get-tuple-element.56), channel_id=1, source_target_pairs={{8,0},{16,8},{24,16},{9,1},{17,9},{25,17},{10,2},{18,10},{26,18},{... | collective-permute-start | bytes 49160 | tf_op jit(solution)/shard_map/ppermute | solution.py:20
  49.8 2.0 %collective-permute-done.8 = f32[1,32,128]{2,1,0:T(8,128)S(1)} collective-permute-done((f32[1,32,128]{2,1,0:T(8,128)S(1)}, f32[1,32,128]{2,1,0:T(8,128)S(1)}, u32[]{:S(2)}, u32[]{:S(2)}) %collective-permute-start.8) | collective-permute-done | bytes 16416 | tf_op jit(solution)/shard_map/ppermute | solution.py:20
  51.8 1.9 %collective-permute-start.10 = (f32[18,1,128]{2,1,0:T(1,128)S(1)}, f32[18,1,128]{2,1,0:T(1,128)S(1)}, u32[]{:S(2)}, u32[]{:S(2)}) collective-permute-start(f32[18,1,128]{2,1,0:T(1,128)S(1)} %get-tuple-element.43), channel_id=1, source_target_pairs={{1,0},{2,1},{3,2},{4,3},{5,4},{6,5},{7,6},{9,8},{10,9},{11,10},{12... | collective-permute-start | bytes 27656 | tf_op jit(solution)/shard_map/ppermute | solution.py:20
  53.8 4.8 %collective-permute-start.11 = (f32[18,1,128]{2,1,0:T(1,128)S(1)}, f32[18,1,128]{2,1,0:T(1,128)S(1)}, u32[]{:S(2)}, u32[]{:S(2)}) collective-permute-start(f32[18,1,128]{2,1,0:T(1,128)S(1)} %get-tuple-element.44), channel_id=1, source_target_pairs={{0,1},{1,2},{2,3},{3,4},{4,5},{5,6},{6,7},{8,9},{9,10},{10,11},{11... | collective-permute-start | bytes 27656 | tf_op jit(solution)/shard_map/ppermute | solution.py:17
  60.4 14.9 %all-reduce.9 = (f32[]{:T(128)}, f32[]{:T(128)}, f32[]{:T(128)}, f32[]{:T(128)}) all-reduce(f32[]{:T(128)} %get-tuple-element.6, f32[]{:T(128)} %get-tuple-element.5, f32[]{:T(128)} %get-tuple-element.4, f32[]{:T(128)} %get-tuple-element.3), channel_id=1, replica_groups=mesh['gy'=4,'gz'=8] {'gz'}, use_global_device_ids=true, to_apply=%region_1.2 | all-reduce | flops 4 | bytes 32 | tf_op jit(solution)/shard_map/psum | solution.py:9
  75.4 7.5 %all-reduce.11 = (f32[]{:T(128)}, f32[]{:T(128)}, f32[]{:T(128)}, f32[]{:T(128)}) all-reduce(f32[]{:T(128)} %get-tuple-element.11, f32[]{:T(128)} %get-tuple-element.12, f32[]{:T(128)} %get-tuple-element.13, f32[]{:T(128)} %get-tuple-element.14), channel_id=1, replica_groups=mesh['gy'=4,'gz'=8] {'gy'}, use_global_device_ids=true, to_apply=%region_2.3 | all-reduce | flops 4 | bytes 32 | tf_op jit(solution)/shard_map/psum | solution.py:9
  85.5 3.2 %collective-permute-start.21 = (f32[1,32,128]{2,1,0:T(8,128)}, f32[1,32,128]{2,1,0:T(8,128)S(1)}, u32[]{:S(2)}, u32[]{:S(2)}) collective-permute-start(f32[1,32,128]{2,1,0:T(8,128)} %get-tuple-element.51), channel_id=1, source_target_pairs={{0,8},{8,16},{16,24},{1,9},{9,17},{17,25},{2,10},{10,18},{18,26},{... | collective-permute-start | bytes 49160 | tf_op jit(solution)/shard_map/ppermute | solution.py:17
  88.7 2.1 %collective-permute-start.20 = (f32[1,32,128]{2,1,0:T(8,128)S(1)}, f32[1,32,128]{2,1,0:T(8,128)S(1)}, u32[]{:S(2)}, u32[]{:S(2)}) collective-permute-start(f32[1,32,128]{2,1,0:T(8,128)S(1)} %get-tuple-element.52), channel_id=1, source_target_pairs={{8,0},{16,8},{24,16},{9,1},{17,9},{25,17},{10,2},{18,10},{26,18},{... | collective-permute-start | bytes 49160 | tf_op jit(solution)/shard_map/ppermute | solution.py:20
  92.9 4.1 %collective-permute-start.13 = (f32[1,32,128]{2,1,0:T(8,128)S(1)}, f32[1,32,128]{2,1,0:T(8,128)S(1)}, u32[]{:S(2)}, u32[]{:S(2)}) collective-permute-start(f32[1,32,128]{2,1,0:T(8,128)S(1)} %get-tuple-element.53), channel_id=1, source_target_pairs={{0,8},{8,16},{16,24},{1,9},{9,17},{17,25},{2,10},{10,18},{18,26},{... | collective-permute-start | bytes 49160 | tf_op jit(solution)/shard_map/ppermute | solution.py:17
  98.9 7.0 %collective-permute-start.22 = (f32[18,1,128]{2,1,0:T(1,128)S(1)}, f32[18,1,128]{2,1,0:T(1,128)S(1)}, u32[]{:S(2)}, u32[]{:S(2)}) collective-permute-start(f32[18,1,128]{2,1,0:T(1,128)S(1)} %get-tuple-element.39), channel_id=1, source_target_pairs={{1,0},{2,1},{3,2},{4,3},{5,4},{6,5},{7,6},{9,8},{10,9},{11,10},{12... | collective-permute-start | bytes 27656 | tf_op jit(solution)/shard_map/ppermute | solution.py:20
  105.9 1.9 %collective-permute-start.23 = (f32[18,1,128]{2,1,0:T(1,128)S(1)}, f32[18,1,128]{2,1,0:T(1,128)S(1)}, u32[]{:S(2)}, u32[]{:S(2)}) collective-permute-start(f32[18,1,128]{2,1,0:T(1,128)S(1)} %get-tuple-element.40), channel_id=1, source_target_pairs={{0,1},{1,2},{2,3},{3,4},{4,5},{5,6},{6,7},{8,9},{9,10},{10,11},{11... | collective-permute-start | bytes 27656 | tf_op jit(solution)/shard_map/ppermute | solution.py:17
  107.9 2.6 %collective-permute-start.14 = (f32[18,1,128]{2,1,0:T(1,128)S(1)}, f32[18,1,128]{2,1,0:T(1,128)S(1)}, u32[]{:S(2)}, u32[]{:S(2)}) collective-permute-start(f32[18,1,128]{2,1,0:T(1,128)S(1)} %get-tuple-element.41), channel_id=1, source_target_pairs={{1,0},{2,1},{3,2},{4,3},{5,4},{6,5},{7,6},{9,8},{10,9},{11,10},{12... | collective-permute-start | bytes 27656 | tf_op jit(solution)/shard_map/ppermute | solution.py:20
  110.5 3.0 %collective-permute-start.15 = (f32[18,1,128]{2,1,0:T(1,128)S(1)}, f32[18,1,128]{2,1,0:T(1,128)S(1)}, u32[]{:S(2)}, u32[]{:S(2)}) collective-permute-start(f32[18,1,128]{2,1,0:T(1,128)S(1)} %get-tuple-element.42), channel_id=1, source_target_pairs={{0,1},{1,2},{2,3},{3,4},{4,5},{5,6},{6,7},{8,9},{9,10},{10,11},{11... | collective-permute-start | bytes 27656 | tf_op jit(solution)/shard_map/ppermute | solution.py:17
  115.5 13.1 %all-reduce.8 = (f32[]{:T(128)}, f32[]{:T(128)}, f32[]{:T(128)}, f32[]{:T(128)}) all-reduce(f32[]{:T(128)} %get-tuple-element.25, f32[]{:T(128)} %fusion.36, f32[]{:T(128)} %get-tuple-element.23, f32[]{:T(128)} %fusion.46), channel_id=1, replica_groups=mesh['gy'=4,'gz'=8] {'gz'}, use_global_device_ids=true, to_apply=%region_7.8 | all-reduce | flops 4 | bytes 32 | tf_op jit(solution)/shard_map/psum | solution.py:9
  128.6 8.0 %all-reduce.10 = (f32[]{:T(128)}, f32[]{:T(128)}, f32[]{:T(128)}, f32[]{:T(128)}) all-reduce(f32[]{:T(128)} %get-tuple-element.7, f32[]{:T(128)} %get-tuple-element.8, f32[]{:T(128)} %get-tuple-element.9, f32[]{:T(128)} %get-tuple-element.10), channel_id=1, replica_groups=mesh['gy'=4,'gz'=8] {'gy'}, use_global_device_ids=true, to_apply=%region_8.9 | all-reduce | flops 4 | bytes 32 | tf_op jit(solution)/shard_map/psum | solution.py:9
  146.1 2.8 %collective-permute-start.24 = (f32[2,1,32,128]{3,2,1,0:T(8,128)S(1)}, f32[2,1,32,128]{3,2,1,0:T(8,128)S(1)}, u32[]{:S(2)}, u32[]{:S(2)}) collective-permute-start(f32[2,1,32,128]{3,2,1,0:T(8,128)S(1)} %get-tuple-element.37), channel_id=1, source_target_pairs={{0,8},{8,16},{16,24},{1,9},{9,17},{17,25},{2,10},{10,18},{18,26},{... | collective-permute-start | bytes 98312 | tf_op jit(solution)/shard_map/ppermute | solution.py:17
  148.9 2.5 %collective-permute-start.25 = (f32[2,1,32,128]{3,2,1,0:T(8,128)S(1)}, f32[2,1,32,128]{3,2,1,0:T(8,128)S(1)}, u32[]{:S(2)}, u32[]{:S(2)}) collective-permute-start(f32[2,1,32,128]{3,2,1,0:T(8,128)S(1)} %get-tuple-element.38), channel_id=1, source_target_pairs={{8,0},{16,8},{24,16},{9,1},{17,9},{25,17},{10,2},{18,10},{26,18},{... | collective-permute-start | bytes 98312 | tf_op jit(solution)/shard_map/ppermute | solution.py:20
  151.4 3.1 %collective-permute-done.25 = f32[2,1,32,128]{3,2,1,0:T(8,128)S(1)} collective-permute-done((f32[2,1,32,128]{3,2,1,0:T(8,128)S(1)}, f32[2,1,32,128]{3,2,1,0:T(8,128)S(1)}, u32[]{:S(2)}, u32[]{:S(2)}) %collective-permute-start.25) | collective-permute-done | bytes 32800 | tf_op jit(solution)/shard_map/ppermute | solution.py:20
  154.5 5.2 %collective-permute-start.26 = (f32[2,18,1,128]{3,2,1,0:T(1,128)S(1)}, f32[2,18,1,128]{3,2,1,0:T(1,128)S(1)}, u32[]{:S(2)}, u32[]{:S(2)}) collective-permute-start(f32[2,18,1,128]{3,2,1,0:T(1,128)S(1)} %get-tuple-element.35), channel_id=1, source_target_pairs={{0,1},{1,2},{2,3},{3,4},{4,5},{5,6},{6,7},{8,9},{9,10},{10,11},{11... | collective-permute-start | bytes 55304 | tf_op jit(solution)/shard_map/ppermute | solution.py:17
  159.7 3.1 %collective-permute-start.27 = (f32[2,18,1,128]{3,2,1,0:T(1,128)S(1)}, f32[2,18,1,128]{3,2,1,0:T(1,128)S(1)}, u32[]{:S(2)}, u32[]{:S(2)}) collective-permute-start(f32[2,18,1,128]{3,2,1,0:T(1,128)S(1)} %get-tuple-element.36), channel_id=1, source_target_pairs={{1,0},{2,1},{3,2},{4,3},{5,4},{6,5},{7,6},{9,8},{10,9},{11,10},{12... | collective-permute-start | bytes 55304 | tf_op jit(solution)/shard_map/ppermute | solution.py:20
  162.8 2.0 %collective-permute-done.27 = f32[2,18,1,128]{3,2,1,0:T(1,128)S(1)} collective-permute-done((f32[2,18,1,128]{3,2,1,0:T(1,128)S(1)}, f32[2,18,1,128]{3,2,1,0:T(1,128)S(1)}, u32[]{:S(2)}, u32[]{:S(2)}) %collective-permute-start.27) | collective-permute-done | bytes 18464 | tf_op jit(solution)/shard_map/ppermute | solution.py:20
  (78 shorter events, 20.5 us)
Async XLA Ops:
  1.4 35.5 %collective-permute-start.4 = (f32[1,32,128]{2,1,0:T(8,128)S(1)}, f32[1,32,128]{2,1,0:T(8,128)S(1)}, u32[]{:S(2)}, u32[]{:S(2)}) collective-permute-start(f32[1,32,128]{2,1,0:T(8,128)S(1)} %get-tuple-element.57), channel_id=1, source_target_pairs={{8,0},{16,8},{24,16},{9,1},{17,9},{25,17},{10,2},{18,10},{26,18},{... | collective-permute-start | bytes 49160 | tf_op jit(solution)/shard_map/ppermute | solution.py:20
  3.3 29.9 %collective-permute-start.5 = (f32[1,32,128]{2,1,0:T(8,128)S(1)}, f32[1,32,128]{2,1,0:T(8,128)S(1)}, u32[]{:S(2)}, u32[]{:S(2)}) collective-permute-start(f32[1,32,128]{2,1,0:T(8,128)S(1)} %get-tuple-element.58), channel_id=1, source_target_pairs={{0,8},{8,16},{16,24},{1,9},{9,17},{17,25},{2,10},{10,18},{18,26},{... | collective-permute-start | bytes 49160 | tf_op jit(solution)/shard_map/ppermute | solution.py:17
  8.3 9.1 %collective-permute-start.1 = (f32[1,32,128]{2,1,0:T(8,128)S(1)}, f32[1,32,128]{2,1,0:T(8,128)S(1)}, u32[]{:S(2)}, u32[]{:S(2)}) collective-permute-start(f32[1,32,128]{2,1,0:T(8,128)S(1)} %get-tuple-element.60), channel_id=1, source_target_pairs={{0,8},{8,16},{16,24},{1,9},{9,17},{17,25},{2,10},{10,18},{18,26},{... | collective-permute-start | bytes 49160 | tf_op jit(solution)/shard_map/ppermute | solution.py:17
  11.2 19.9 %collective-permute-start.16 = (f32[1,32,128]{2,1,0:T(8,128)S(1)}, f32[1,32,128]{2,1,0:T(8,128)S(1)}, u32[]{:S(2)}, u32[]{:S(2)}) collective-permute-start(f32[1,32,128]{2,1,0:T(8,128)S(1)} %get-tuple-element.61), channel_id=1, source_target_pairs={{8,0},{16,8},{24,16},{9,1},{17,9},{25,17},{10,2},{18,10},{26,18},{... | collective-permute-start | bytes 49160 | tf_op jit(solution)/shard_map/ppermute | solution.py:20
  14.3 14.9 %collective-permute-start.17 = (f32[1,32,128]{2,1,0:T(8,128)S(1)}, f32[1,32,128]{2,1,0:T(8,128)S(1)}, u32[]{:S(2)}, u32[]{:S(2)}) collective-permute-start(f32[1,32,128]{2,1,0:T(8,128)S(1)} %get-tuple-element.62), channel_id=1, source_target_pairs={{0,8},{8,16},{16,24},{1,9},{9,17},{17,25},{2,10},{10,18},{18,26},{... | collective-permute-start | bytes 49160 | tf_op jit(solution)/shard_map/ppermute | solution.py:17
  17.4 5.4 %collective-permute-start = (f32[1,32,128]{2,1,0:T(8,128)S(1)}, f32[1,32,128]{2,1,0:T(8,128)S(1)}, u32[]{:S(2)}, u32[]{:S(2)}) collective-permute-start(f32[1,32,128]{2,1,0:T(8,128)S(1)} %get-tuple-element.59), channel_id=1, source_target_pairs={{8,0},{16,8},{24,16},{9,1},{17,9},{25,17},{10,2},{18,10},{26,18},{... | collective-permute-start | bytes 49160 | tf_op jit(solution)/shard_map/ppermute | solution.py:20
  19.6 11.5 %copy-start.2 = (f32[16,32,128]{2,1,0:T(8,128)S(1)}, f32[16,32,128]{2,1,0:T(8,128)}, u32[]{:S(2)}) copy-start(f32[16,32,128]{2,1,0:T(8,128)} %param.9) | copy-start | bytes 786436
  22.8 16.1 %collective-permute-start.3 = (f32[18,1,128]{2,1,0:T(1,128)S(1)}, f32[18,1,128]{2,1,0:T(1,128)S(1)}, u32[]{:S(2)}, u32[]{:S(2)}) collective-permute-start(f32[18,1,128]{2,1,0:T(1,128)S(1)} %get-tuple-element.47), channel_id=1, source_target_pairs={{0,1},{1,2},{2,3},{3,4},{4,5},{5,6},{6,7},{8,9},{9,10},{10,11},{11... | collective-permute-start | bytes 27656 | tf_op jit(solution)/shard_map/ppermute | solution.py:17
  29.2 13.6 %collective-permute-start.2 = (f32[18,1,128]{2,1,0:T(1,128)S(1)}, f32[18,1,128]{2,1,0:T(1,128)S(1)}, u32[]{:S(2)}, u32[]{:S(2)}) collective-permute-start(f32[18,1,128]{2,1,0:T(1,128)S(1)} %get-tuple-element.48), channel_id=1, source_target_pairs={{1,0},{2,1},{3,2},{4,3},{5,4},{6,5},{7,6},{9,8},{10,9},{11,10},{12... | collective-permute-start | bytes 27656 | tf_op jit(solution)/shard_map/ppermute | solution.py:20
  31.2 11.6 %collective-permute-start.18 = (f32[18,1,128]{2,1,0:T(1,128)S(1)}, f32[18,1,128]{2,1,0:T(1,128)S(1)}, u32[]{:S(2)}, u32[]{:S(2)}) collective-permute-start(f32[18,1,128]{2,1,0:T(1,128)S(1)} %get-tuple-element.49), channel_id=1, source_target_pairs={{1,0},{2,1},{3,2},{4,3},{5,4},{6,5},{7,6},{9,8},{10,9},{11,10},{12... | collective-permute-start | bytes 27656 | tf_op jit(solution)/shard_map/ppermute | solution.py:20
  33.2 9.7 %collective-permute-start.19 = (f32[18,1,128]{2,1,0:T(1,128)S(1)}, f32[18,1,128]{2,1,0:T(1,128)S(1)}, u32[]{:S(2)}, u32[]{:S(2)}) collective-permute-start(f32[18,1,128]{2,1,0:T(1,128)S(1)} %get-tuple-element.50), channel_id=1, source_target_pairs={{0,1},{1,2},{2,3},{3,4},{4,5},{5,6},{6,7},{8,9},{9,10},{10,11},{11... | collective-permute-start | bytes 27656 | tf_op jit(solution)/shard_map/ppermute | solution.py:17
  36.8 6.0 %copy-start = (f32[16,32,128]{2,1,0:T(8,128)S(1)}, f32[16,32,128]{2,1,0:T(8,128)}, u32[]{:S(2)}) copy-start(f32[16,32,128]{2,1,0:T(8,128)} %param.5) | copy-start | bytes 786436
  36.9 7.2 %collective-permute-start.6 = (f32[18,1,128]{2,1,0:T(1,128)S(1)}, f32[18,1,128]{2,1,0:T(1,128)S(1)}, u32[]{:S(2)}, u32[]{:S(2)}) collective-permute-start(f32[18,1,128]{2,1,0:T(1,128)S(1)} %get-tuple-element.45), channel_id=1, source_target_pairs={{1,0},{2,1},{3,2},{4,3},{5,4},{6,5},{7,6},{9,8},{10,9},{11,10},{12... | collective-permute-start | bytes 27656 | tf_op jit(solution)/shard_map/ppermute | solution.py:20
  39.0 5.1 %collective-permute-start.7 = (f32[18,1,128]{2,1,0:T(1,128)S(1)}, f32[18,1,128]{2,1,0:T(1,128)S(1)}, u32[]{:S(2)}, u32[]{:S(2)}) collective-permute-start(f32[18,1,128]{2,1,0:T(1,128)S(1)} %get-tuple-element.46), channel_id=1, source_target_pairs={{0,1},{1,2},{2,3},{3,4},{4,5},{5,6},{6,7},{8,9},{9,10},{10,11},{11... | collective-permute-start | bytes 27656 | tf_op jit(solution)/shard_map/ppermute | solution.py:17
  44.5 5.3 %collective-permute-start.9 = (f32[1,32,128]{2,1,0:T(8,128)S(1)}, f32[1,32,128]{2,1,0:T(8,128)S(1)}, u32[]{:S(2)}, u32[]{:S(2)}) collective-permute-start(f32[1,32,128]{2,1,0:T(8,128)S(1)} %get-tuple-element.55), channel_id=1, source_target_pairs={{0,8},{8,16},{16,24},{1,9},{9,17},{17,25},{2,10},{10,18},{18,26},{... | collective-permute-start | bytes 49160 | tf_op jit(solution)/shard_map/ppermute | solution.py:17
  46.4 5.4 %collective-permute-start.8 = (f32[1,32,128]{2,1,0:T(8,128)S(1)}, f32[1,32,128]{2,1,0:T(8,128)S(1)}, u32[]{:S(2)}, u32[]{:S(2)}) collective-permute-start(f32[1,32,128]{2,1,0:T(8,128)S(1)} %get-tuple-element.56), channel_id=1, source_target_pairs={{8,0},{16,8},{24,16},{9,1},{17,9},{25,17},{10,2},{18,10},{26,18},{... | collective-permute-start | bytes 49160 | tf_op jit(solution)/shard_map/ppermute | solution.py:20
  51.8 6.8 %collective-permute-start.10 = (f32[18,1,128]{2,1,0:T(1,128)S(1)}, f32[18,1,128]{2,1,0:T(1,128)S(1)}, u32[]{:S(2)}, u32[]{:S(2)}) collective-permute-start(f32[18,1,128]{2,1,0:T(1,128)S(1)} %get-tuple-element.43), channel_id=1, source_target_pairs={{1,0},{2,1},{3,2},{4,3},{5,4},{6,5},{7,6},{9,8},{10,9},{11,10},{12... | collective-permute-start | bytes 27656 | tf_op jit(solution)/shard_map/ppermute | solution.py:20
  53.8 5.6 %collective-permute-start.11 = (f32[18,1,128]{2,1,0:T(1,128)S(1)}, f32[18,1,128]{2,1,0:T(1,128)S(1)}, u32[]{:S(2)}, u32[]{:S(2)}) collective-permute-start(f32[18,1,128]{2,1,0:T(1,128)S(1)} %get-tuple-element.44), channel_id=1, source_target_pairs={{0,1},{1,2},{2,3},{3,4},{4,5},{5,6},{6,7},{8,9},{9,10},{10,11},{11... | collective-permute-start | bytes 27656 | tf_op jit(solution)/shard_map/ppermute | solution.py:17
  85.5 13.3 %collective-permute-start.21 = (f32[1,32,128]{2,1,0:T(8,128)}, f32[1,32,128]{2,1,0:T(8,128)S(1)}, u32[]{:S(2)}, u32[]{:S(2)}) collective-permute-start(f32[1,32,128]{2,1,0:T(8,128)} %get-tuple-element.51), channel_id=1, source_target_pairs={{0,8},{8,16},{16,24},{1,9},{9,17},{17,25},{2,10},{10,18},{18,26},{... | collective-permute-start | bytes 49160 | tf_op jit(solution)/shard_map/ppermute | solution.py:17
  88.7 10.2 %collective-permute-start.20 = (f32[1,32,128]{2,1,0:T(8,128)S(1)}, f32[1,32,128]{2,1,0:T(8,128)S(1)}, u32[]{:S(2)}, u32[]{:S(2)}) collective-permute-start(f32[1,32,128]{2,1,0:T(8,128)S(1)} %get-tuple-element.52), channel_id=1, source_target_pairs={{8,0},{16,8},{24,16},{9,1},{17,9},{25,17},{10,2},{18,10},{26,18},{... | collective-permute-start | bytes 49160 | tf_op jit(solution)/shard_map/ppermute | solution.py:20
  92.9 15.0 %collective-permute-start.13 = (f32[1,32,128]{2,1,0:T(8,128)S(1)}, f32[1,32,128]{2,1,0:T(8,128)S(1)}, u32[]{:S(2)}, u32[]{:S(2)}) collective-permute-start(f32[1,32,128]{2,1,0:T(8,128)S(1)} %get-tuple-element.53), channel_id=1, source_target_pairs={{0,8},{8,16},{16,24},{1,9},{9,17},{17,25},{2,10},{10,18},{18,26},{... | collective-permute-start | bytes 49160 | tf_op jit(solution)/shard_map/ppermute | solution.py:17
  96.9 10.9 %collective-permute-start.12 = (f32[1,32,128]{2,1,0:T(8,128)S(1)}, f32[1,32,128]{2,1,0:T(8,128)S(1)}, u32[]{:S(2)}, u32[]{:S(2)}) collective-permute-start(f32[1,32,128]{2,1,0:T(8,128)S(1)} %get-tuple-element.54), channel_id=1, source_target_pairs={{8,0},{16,8},{24,16},{9,1},{17,9},{25,17},{10,2},{18,10},{26,18},{... | collective-permute-start | bytes 49160 | tf_op jit(solution)/shard_map/ppermute | solution.py:20
  98.9 14.6 %collective-permute-start.22 = (f32[18,1,128]{2,1,0:T(1,128)S(1)}, f32[18,1,128]{2,1,0:T(1,128)S(1)}, u32[]{:S(2)}, u32[]{:S(2)}) collective-permute-start(f32[18,1,128]{2,1,0:T(1,128)S(1)} %get-tuple-element.39), channel_id=1, source_target_pairs={{1,0},{2,1},{3,2},{4,3},{5,4},{6,5},{7,6},{9,8},{10,9},{11,10},{12... | collective-permute-start | bytes 27656 | tf_op jit(solution)/shard_map/ppermute | solution.py:20
  105.9 7.6 %collective-permute-start.23 = (f32[18,1,128]{2,1,0:T(1,128)S(1)}, f32[18,1,128]{2,1,0:T(1,128)S(1)}, u32[]{:S(2)}, u32[]{:S(2)}) collective-permute-start(f32[18,1,128]{2,1,0:T(1,128)S(1)} %get-tuple-element.40), channel_id=1, source_target_pairs={{0,1},{1,2},{2,3},{3,4},{4,5},{5,6},{6,7},{8,9},{9,10},{10,11},{11... | collective-permute-start | bytes 27656 | tf_op jit(solution)/shard_map/ppermute | solution.py:17
  107.9 6.6 %collective-permute-start.14 = (f32[18,1,128]{2,1,0:T(1,128)S(1)}, f32[18,1,128]{2,1,0:T(1,128)S(1)}, u32[]{:S(2)}, u32[]{:S(2)}) collective-permute-start(f32[18,1,128]{2,1,0:T(1,128)S(1)} %get-tuple-element.41), channel_id=1, source_target_pairs={{1,0},{2,1},{3,2},{4,3},{5,4},{6,5},{7,6},{9,8},{10,9},{11,10},{12... | collective-permute-start | bytes 27656 | tf_op jit(solution)/shard_map/ppermute | solution.py:20
  110.5 4.0 %collective-permute-start.15 = (f32[18,1,128]{2,1,0:T(1,128)S(1)}, f32[18,1,128]{2,1,0:T(1,128)S(1)}, u32[]{:S(2)}, u32[]{:S(2)}) collective-permute-start(f32[18,1,128]{2,1,0:T(1,128)S(1)} %get-tuple-element.42), channel_id=1, source_target_pairs={{0,1},{1,2},{2,3},{3,4},{4,5},{5,6},{6,7},{8,9},{9,10},{10,11},{11... | collective-permute-start | bytes 27656 | tf_op jit(solution)/shard_map/ppermute | solution.py:17
  146.0 18.8 %copy-start.3 = (f32[16,32,128]{2,1,0:T(8,128)}, f32[16,32,128]{2,1,0:T(8,128)S(1)}, u32[]{:S(2)}) copy-start(f32[16,32,128]{2,1,0:T(8,128)S(1)} %get-tuple-element.63) | copy-start | bytes 786436
  146.0 18.7 %copy-start.4 = (f32[16,32,128]{2,1,0:T(8,128)}, f32[16,32,128]{2,1,0:T(8,128)S(1)}, u32[]{:S(2)}) copy-start(f32[16,32,128]{2,1,0:T(8,128)S(1)} %get-tuple-element.64) | copy-start | bytes 786436
  146.1 5.3 %collective-permute-start.24 = (f32[2,1,32,128]{3,2,1,0:T(8,128)S(1)}, f32[2,1,32,128]{3,2,1,0:T(8,128)S(1)}, u32[]{:S(2)}, u32[]{:S(2)}) collective-permute-start(f32[2,1,32,128]{3,2,1,0:T(8,128)S(1)} %get-tuple-element.37), channel_id=1, source_target_pairs={{0,8},{8,16},{16,24},{1,9},{9,17},{17,25},{2,10},{10,18},{18,26},{... | collective-permute-start | bytes 98312 | tf_op jit(solution)/shard_map/ppermute | solution.py:17
  148.9 5.6 %collective-permute-start.25 = (f32[2,1,32,128]{3,2,1,0:T(8,128)S(1)}, f32[2,1,32,128]{3,2,1,0:T(8,128)S(1)}, u32[]{:S(2)}, u32[]{:S(2)}) collective-permute-start(f32[2,1,32,128]{3,2,1,0:T(8,128)S(1)} %get-tuple-element.38), channel_id=1, source_target_pairs={{8,0},{16,8},{24,16},{9,1},{17,9},{25,17},{10,2},{18,10},{26,18},{... | collective-permute-start | bytes 98312 | tf_op jit(solution)/shard_map/ppermute | solution.py:20
  154.5 8.3 %collective-permute-start.26 = (f32[2,18,1,128]{3,2,1,0:T(1,128)S(1)}, f32[2,18,1,128]{3,2,1,0:T(1,128)S(1)}, u32[]{:S(2)}, u32[]{:S(2)}) collective-permute-start(f32[2,18,1,128]{3,2,1,0:T(1,128)S(1)} %get-tuple-element.35), channel_id=1, source_target_pairs={{0,1},{1,2},{2,3},{3,4},{4,5},{5,6},{6,7},{8,9},{9,10},{10,11},{11... | collective-permute-start | bytes 55304 | tf_op jit(solution)/shard_map/ppermute | solution.py:17
  159.7 5.1 %collective-permute-start.27 = (f32[2,18,1,128]{3,2,1,0:T(1,128)S(1)}, f32[2,18,1,128]{3,2,1,0:T(1,128)S(1)}, u32[]{:S(2)}, u32[]{:S(2)}) collective-permute-start(f32[2,18,1,128]{3,2,1,0:T(1,128)S(1)} %get-tuple-element.36), channel_id=1, source_target_pairs={{1,0},{2,1},{3,2},{4,3},{5,4},{6,5},{7,6},{9,8},{10,9},{11,10},{12... | collective-permute-start | bytes 55304 | tf_op jit(solution)/shard_map/ppermute | solution.py:20
  (3 other events, 16.8 us)
